TPU v7x, 32 devices: a whole 2x2x4 slice. The times are simulated.
32 devices in a mesh: row: 4 (over z), col: 8 (over y, x, core).
Axes of the slice: x: 2, y: 2, z: 4, core: 2. Of those that a mesh axis runs over, the one named last changes fastest.
Arguments:
- matrix: float32 [4, 1024, 2, 2048], P(None, 'row', None, 'col'), may hold values from -6 to 6, as said below
Outputs:
- factored: float32 [4, 1024, 2, 2048], P(None, 'row', None, 'col')
Inputs may be any that keep to these rules, and one draw needn't show every extreme that they name: symmetric; the leading 2 * 256 rows and columns form a positive definite matrix.
All inputs are finite; a program needn't handle non-finite values.
Results may differ from a plain program's by a relative error of at most 0.0001.
Values sent between devices are 32-bit elements; how exact they have to be, the bound alone decides.
A program may use at most 64 MiB of HBM per device.

v0:
```python
import jax
import jax.numpy as jnp
from jax import lax
from jax.sharding import PartitionSpec as P

PANELS = 2


def spread(block, axis, source):
    block = jnp.where(lax.axis_index(axis) == source, block, jnp.zeros_like(block))
    return lax.psum(block, axis)


def shards(matrix):
    row_count = lax.axis_size("row")
    col_count = lax.axis_size("col")
    row_index = lax.axis_index("row")
    col_index = lax.axis_index("col")
    row_blocks = matrix.shape[0]
    col_blocks = matrix.shape[2]
    width = matrix.shape[1]
    global_rows = jnp.arange(row_blocks, dtype=jnp.int32) * row_count + row_index
    global_cols = jnp.arange(col_blocks, dtype=jnp.int32) * col_count + col_index
    stride = col_count // row_count
    picked = jnp.arange(col_blocks, dtype=jnp.int32) * stride + col_index // row_count

    def solve_rows(diag_factor, column, panel):
        flat = column.reshape(-1, width)
        solved = lax.linalg.triangular_solve(
            diag_factor, flat, left_side=False, lower=True, transpose_a=True
        )
        solved = solved.reshape(column.shape)
        block_ids = global_rows[:, None, None]
        return jnp.where(
            block_ids < panel, 0.0, jnp.where(block_ids == panel, diag_factor[None], solved)
        )

    def factor_panel(work, panel):
        local_row = panel // row_count
        local_col = panel // col_count
        owner = (row_index == panel % row_count) & (col_index == panel % col_count)
        identity = jnp.eye(width, dtype=jnp.float32)
        safe = jnp.where(owner, work[local_row, :, local_col, :], identity)
        column = work[:, :, local_col, :]
        diag_factor = spread(jnp.linalg.cholesky(safe), "row", panel % row_count)
        lower = spread(solve_rows(diag_factor, column, panel), "col", panel % col_count)
        across = spread(lower[picked], "row", col_index % row_count)
        return (lower, across)

    def update_blocks(part, lower, across_part, panel, cols_part):
        product = jnp.einsum(
            "apk,cqk->apcq",
            lower,
            across_part,
            precision=lax.Precision.HIGHEST,
            preferred_element_type=jnp.float32,
        )
        row_ids = global_rows[:, None, None, None]
        col_ids = cols_part[None, None, :, None]
        trailing = jnp.where(row_ids > panel, part - product, 0.0)
        return jnp.where(
            col_ids == panel, lower[:, :, None, :], jnp.where(col_ids > panel, trailing, part)
        )

    work = matrix
    lower, across = factor_panel(work, 0)
    for panel in range(PANELS):
        if panel + 1 < PANELS:
            near = (panel + 1) // col_count
            head = update_blocks(work[:, :, :near], lower, across[:near], panel, global_cols[:near])
            middle = update_blocks(
                work[:, :, near : near + 1],
                lower,
                across[near : near + 1],
                panel,
                global_cols[near : near + 1],
            )
            sectioned = jnp.concatenate((work[:, :, :near], middle, work[:, :, near + 1 :]), axis=2)
            following = factor_panel(sectioned, panel + 1)
            tail = update_blocks(
                work[:, :, near + 1 :], lower, across[near + 1 :], panel, global_cols[near + 1 :]
            )
            work = jnp.concatenate((head, middle, tail), axis=2)
            lower, across = following
        else:
            work = update_blocks(work, lower, across, panel, global_cols)
    return work


def solution(mesh):
    in_specs = (P(None, "row", None, "col"),)
    out_specs = P(None, "row", None, "col")
    return jax.shard_map(shards, mesh=mesh, in_specs=in_specs, out_specs=out_specs, check_vma=False)
```

profile of v0, /device:TPU:0, one launch (start us, length us, event | category | flops | bytes accessed | tf_op | source)
XLA Modules:
  0.0 433.3 jit_solution(13667151102278012887)
XLA Ops:
  6.5 1.2 slice.64
  8.2 11.7 %cholesky.130 = f32[128,128]{1,0:T(8,128)S(1)} custom-call(f32[128,128]{1,0:T(8,128)S(1)} %cholesky.194), custom_call_target="Cholesky" | custom-call | tf_op jit(solution)/shard_map/jit(cholesky)/cholesky | solution.py:45
  19.9 9.8 %custom-call.13 = f32[1,128,128]{1,2,0:T(8,128)S(1)} custom-call(f32[1,128,128]{2,1,0:T(8,128)S(1)} %get-tuple-element.52), custom_call_target="InvertDiagBlocksLowerTriangular" | custom-call | tf_op jit(solution)/shard_map/jit(cholesky)/cholesky | solution.py:45
  30.2 11.7 %cholesky.147 = f32[128,128]{1,0:T(8,128)S(1)} custom-call(f32[128,128]{1,0:T(8,128)S(1)} %convolution_subtract_fusion.3), custom_call_target="Cholesky" | custom-call | tf_op jit(solution)/shard_map/jit(cholesky)/cholesky | solution.py:45
  45.0 2.6 fusion.37
  47.7 35.6 %all-reduce.8.cloned.1.call-done = f32[256,256]{1,0:T(8,128)} async-done(((f32[256,256]{1,0:T(8,128)}), f32[256,256]{1,0:T(8,128)}) %all-reduce.8.cloned.1.call-update) | async-done | bytes 262160 | tf_op jit(solution)/shard_map/psum | solution.py:11
  84.3 4.0 while.4
  85.0 1.3 bitcast_dynamic-update-slice_fusion.4
  87.0 1.3 bitcast_dynamic-update-slice_fusion.4
  89.0 19.7 %custom-call.14 = f32[2,128,128]{1,2,0:T(8,128)S(1)} custom-call(f32[2,128,128]{2,1,0:T(8,128)S(1)} %get-tuple-element.21), custom_call_target="InvertDiagBlocksLowerTriangular" | custom-call | tf_op jit(solution)/shard_map/triangular_solve/custom-call.0 | solution.py:29
  113.5 56.6 %all-reduce.10.cloned.1.call-done = f32[4,256,256]{1,2,0:T(8,128)} async-done(((f32[4,256,256]{1,2,0:T(8,128)}), f32[4,256,256]{1,2,0:T(8,128)}) %all-reduce.10.cloned.1.call-update) | async-done | bytes 1048592 | tf_op jit(solution)/shard_map/psum | solution.py:11
  170.1 1.8 gather_fusion
  175.6 35.2 %all-reduce.12.cloned.1.call-done = f32[2,256,256]{1,2,0:T(8,128)} async-done(((f32[2,256,256]{1,2,0:T(8,128)}), f32[2,256,256]{1,2,0:T(8,128)}) %all-reduce.12.cloned.1.call-update) | async-done | bytes 524304 | tf_op jit(solution)/shard_map/psum | solution.py:11
  210.9 2.1 fusion.3
  213.3 11.7 %cholesky.164 = f32[128,128]{1,0:T(8,128)S(1)} custom-call(f32[128,128]{1,0:T(8,128)S(1)} %cholesky.197), custom_call_target="Cholesky" | custom-call | tf_op jit(solution)/shard_map/jit(cholesky)/cholesky | solution.py:45
  225.7 9.8 %custom-call.15 = f32[1,128,128]{1,2,0:T(8,128)S(1)} custom-call(f32[1,128,128]{2,1,0:T(8,128)S(1)} %get-tuple-element.48), custom_call_target="InvertDiagBlocksLowerTriangular" | custom-call | tf_op jit(solution)/shard_map/jit(cholesky)/cholesky | solution.py:45
  236.1 11.7 %cholesky.181 = f32[128,128]{1,0:T(8,128)S(1)} custom-call(f32[128,128]{1,0:T(8,128)S(1)} %convolution_subtract_fusion.2), custom_call_target="Cholesky" | custom-call | tf_op jit(solution)/shard_map/jit(cholesky)/cholesky | solution.py:45
  251.1 34.9 %all-reduce.14.cloned.1.call-done = f32[256,256]{1,0:T(8,128)} async-done(((f32[256,256]{1,0:T(8,128)}), f32[256,256]{1,0:T(8,128)}) %all-reduce.14.cloned.1.call-update) | async-done | bytes 262160 | tf_op jit(solution)/shard_map/psum | solution.py:11
  287.0 5.3 %while.5 = (s32[]{:T(128)}, f32[256,256]{1,0:T(8,128)S(1)}, s32[2,2]{1,0:T(2,128)}, f32[2,128,128]{2,1,0:T(8,128)S(1)}, s32[]{:T(128)}) while((s32[]{:T(128)}, f32[256,256]{1,0:T(8,128)S(1)}, s32[2,2]{1,0:T(2,128)}, f32[2,128,128]{2,1,0:T(8,128)S(1)}, s32[]{:T(128)}) %tuple.66), condition=%wide.while_cond.clone, body=%wide.while_body.clone.sunk | while | flops 2 | bytes 131189 | solution.py:29
  288.3 1.3 bitcast_dynamic-update-slice_fusion.5
  291.0 1.3 bitcast_dynamic-update-slice_fusion.5
  293.0 20.5 %custom-call.16 = f32[2,128,128]{1,2,0:T(8,128)S(1)} custom-call(f32[2,128,128]{2,1,0:T(8,128)} %copy-done.3), custom_call_target="InvertDiagBlocksLowerTriangular" | custom-call | tf_op jit(solution)/shard_map/triangular_solve/custom-call.0 | solution.py:29
  315.9 1.3 copy.32
  317.2 1.6 copy.33
  322.3 2.3 copy.58
  324.6 53.2 %all-reduce.16.cloned.1.call-done = f32[4,256,256]{1,2,0:T(8,128)} async-done(((f32[4,256,256]{1,2,0:T(8,128)}), f32[4,256,256]{1,2,0:T(8,128)}) %all-reduce.16.cloned.1.call-update) | async-done | bytes 1048592 | tf_op jit(solution)/shard_map/psum | solution.py:11
  377.8 2.6 gather_fusion.1
  380.4 1.9 broadcast_select_fusion
  382.4 3.1 fusion.7
  385.5 33.9 %all-reduce.18.cloned.1.call-done = f32[2,256,256]{1,2,0:T(8,128)} async-done(((f32[2,256,256]{1,2,0:T(8,128)}), f32[2,256,256]{1,2,0:T(8,128)}) %all-reduce.18.cloned.1.call-update) | async-done | bytes 524304 | tf_op jit(solution)/shard_map/psum | solution.py:11
  419.4 4.2 select_select_fusion
  423.7 2.3 copy.41
  (87 shorter events, 25.2 us)
Async XLA Ops:
  6.5 76.8 %all-reduce.8.cloned.1.call-start = ((), (), s32[]{:S(2)}) async-start(), calls=%async_computation | async-start | bytes 524288 | tf_op jit(solution)/shard_map/psum | solution.py:11
  7.8 37.3 %copy-start.1 = (f32[4,256,2,256]{3,2,1,0:T(2,128)S(1)}, f32[4,256,2,256]{3,2,1,0:T(2,128)}, u32[]{:S(2)}) copy-start(f32[4,256,2,256]{3,2,1,0:T(2,128)} %param.4) | copy-start | bytes 6291460
  44.8 125.3 %all-reduce.10.cloned.1.call-start = ((), (), s32[]{:S(2)}) async-start(), calls=%async_computation.1 | async-start | bytes 2097152 | tf_op jit(solution)/shard_map/psum | solution.py:11
  88.4 0.6 copy-start.4
  111.0 1.0 copy-start.2
  113.4 97.5 %all-reduce.12.cloned.1.call-start = ((), (), s32[]{:S(2)}) async-start(), calls=%async_computation.2 | async-start | bytes 1048576 | tf_op jit(solution)/shard_map/psum | solution.py:11
  171.9 38.9 %copy-start = (f32[4,256,256]{1,2,0:T(8,128)S(1)}, f32[4,256,256]{1,2,0:T(8,128)}, u32[]{:S(2)}) copy-start(f32[4,256,256]{1,2,0:T(8,128)} %all-reduce.10.cloned.1.call-done) | copy-start | bytes 3145732
  172.8 113.2 %all-reduce.14.cloned.1.call-start = ((), (), s32[]{:S(2)}) async-start(), calls=%async_computation.3 | async-start | bytes 524288 | tf_op jit(solution)/shard_map/psum | solution.py:11
  250.5 127.4 %all-reduce.16.cloned.1.call-start = ((), (), s32[]{:S(2)}) async-start(), calls=%async_computation.4 | async-start | bytes 2097152 | tf_op jit(solution)/shard_map/psum | solution.py:11
  292.3 0.6 copy-start.3
  321.1 98.4 %all-reduce.18.cloned.1.call-start = ((), (), s32[]{:S(2)}) async-start(), calls=%async_computation.5 | async-start | bytes 1048576 | tf_op jit(solution)/shard_map/psum | solution.py:11
Sparse Core Ops, SparseCore 0:
  44.9 38.3 all-reduce.7
  113.5 56.5 all-reduce.9
  172.9 37.8 all-reduce.11
  250.6 35.4 all-reduce.13
  321.2 56.5 all-reduce.15
  382.5 36.9 all-reduce.17
where the time goes:
time: 442 us; the launch traced here: 433 us
  waiting for transfers between devices  250 us (57%)
  other arithmetic  118 us (27%)
  local copies, waits for them, and re-layouts  30.6 us (7%)
  between operations  19.4 us (4%)
  matrix products  15 us (3%)
    psum x6, waiting for transfers between devices, spread(): return lax.psum(block, axis)  250 us
    another operation x13, other arithmetic, factor_panel(): diag_factor = spread(jnp.linalg.cholesky(safe), 'row', panel % row_count)  68.7 us
    another operation x7, other arithmetic, solve_rows(): lax.linalg.triangular_solve(diag_factor, flat, left_side=False, lower=Tru...  42.3 us
    another operation x17, local copies, waits for them, and re-layouts, solve_rows(): lax.linalg.triangular_solve(diag_factor, flat, left_side=False, lower=Tru...  11 us
    dot_general x3, matrix products, update_blocks(): jnp.einsum('apk,cqk->apcq', lower, across_part, precision=lax.Precision.H...  9.5 us
  transfers between devices with their start and end apart: 6, of which 6 were waited for; matrix products, arithmetic and copies ran while one was open for 2% of the time, Pallas kernels for 0%

commit v1 on v0

v1 whole, which is shorter than its diff:
```python
import functools
import math

import jax
import jax.numpy as jnp
from jax import lax
from jax.experimental import pallas as pl
from jax.experimental.pallas import tpu as pltpu
from jax.sharding import PartitionSpec as P

MESH = pl.DeviceIdType.MESH
PANELS = 2
PIECES = 2
GROUP = 8
HIGHEST = lax.Precision.HIGHEST


def mm(a, b):
    return jnp.dot(a, b, precision=HIGHEST, preferred_element_type=jnp.float32)


def mm_nt(a, b):
    return lax.dot_general(
        a, b, (((1,), (1,)), ((), ())), precision=HIGHEST, preferred_element_type=jnp.float32
    )


def mm_tn(a, b):
    return lax.dot_general(
        a, b, (((0,), (0,)), ((), ())), precision=HIGHEST, preferred_element_type=jnp.float32
    )


def snake(pos, width):
    major, minor = pos // width, pos % width
    return major, jnp.where(major % 2 == 0, minor, width - 1 - minor)


def exchange(shape, m_ref, cols, rows, lead, x_send, x_recv, p_send, p_recv, l_up, l_down, l_recv,
             lp_send, lp_recv, r_up, r_down, r_recv):
    n_row, n_col = shape
    chips = n_col // 2
    width = math.isqrt(chips)
    if width * width != chips:
        width = chips
    height = chips // width
    z = lax.axis_index("row")
    col = lax.axis_index("col")
    chip, core = col // 2, col % 2
    partner = (z, chip * 2 + 1 - core)
    y, x = chip // width, chip % width
    pos_a = y * width + jnp.where(y % 2 == 0, x, width - 1 - x)
    pos_b = x * height + jnp.where(x % 2 == 0, y, height - 1 - y)
    pos = jnp.where(core == 0, pos_a, pos_b)

    def chip_at(p):
        ya, xa = snake(p, width)
        xb, yb = snake(p, height)
        return jnp.where(core == 0, ya * width + xa, yb * width + xb)

    last = chips - 1
    has_next, has_prev = pos < last, pos > 0
    nxt = (z, chip_at(jnp.minimum(pos + 1, last)) * 2 + core)
    prv = (z, chip_at(jnp.maximum(pos - 1, 0)) * 2 + core)
    up, down = (z + 1, col), (z - 1, col)
    has_up, has_down = z < n_row - 1, z > 0

    barrier = pltpu.get_barrier_semaphore()

    def greet(cond, dev):
        @pl.when(cond)
        def _():
            pl.semaphore_signal(barrier, inc=1, device_id=dev, device_id_type=MESH)

    pl.semaphore_signal(barrier, inc=1, device_id=partner, device_id_type=MESH)
    greet(has_next, nxt)
    greet(has_prev, prv)
    greet(has_up, up)
    greet(has_down, down)
    one = lambda c: jnp.where(c, 1, 0)
    pl.semaphore_wait(barrier, 1 + one(has_next) + one(has_prev) + one(has_up) + one(has_down))

    def rcopy(src, dst, s, r, dev):
        return pltpu.make_async_remote_copy(
            src_ref=src, dst_ref=dst, send_sem=s, recv_sem=r, device_id=dev, device_id_type=MESH
        )

    blocks, size = m_ref.shape[0], m_ref.shape[2]
    step = size // PIECES

    def part(t):
        return t // PIECES, pl.ds((t % PIECES) * step, step)

    def x_copies(t, own):
        a, d = part(t)
        src = m_ref.at[a, 0, d] if own else cols.at[core, a, d]
        dst = cols.at[core, a, d]
        return (rcopy(src, dst, x_send.at[t], x_recv.at[t], nxt),
                rcopy(src, dst, p_send.at[t], p_recv.at[t], partner))

    def x_piece(t):
        @pl.when(jnp.logical_not(has_prev))
        def _():
            chain, side = x_copies(t, True)
            chain.start()
            side.start()

        @pl.when(has_prev)
        def _():
            chain, side = x_copies(t, False)
            chain.wait_recv()

            @pl.when(has_next)
            def _():
                chain.start()
            side.start()

    def r_copy(k, u, own, is_up):
        c, d = part(u)
        src = m_ref.at[0, c, d] if own else rows.at[k, c, d]
        sem = r_up.at[k, u] if is_up else r_down.at[u]
        return rcopy(src, rows.at[k, c, d], sem, r_recv.at[k, u], up if is_up else down)

    n_r = m_ref.shape[1] * PIECES

    def r_start(u):
        @pl.when(z == 0)
        def _():
            r_copy(0, u, True, True).start()

        @pl.when(z == 1)
        def _():
            r_copy(1, u, True, False).start()

            @pl.when(has_up)
            def _():
                r_copy(1, u, True, True).start()

    def r_relay(k, u):
        @pl.when(z != k)
        def _():
            r_copy(k, u, False, True).wait_recv()

        @pl.when((z > k) & has_up)
        def _():
            r_copy(k, u, False, True).start()

    origin = (0, 1, 1)
    carrier = (0, 0, 1)

    def l_copy(b, own, is_up):
        src = cols.at[carrier[b], 0] if own == 2 else (m_ref.at[0, 0] if own == 1 else lead.at[b])
        sem = l_up.at[b] if is_up else l_down.at[b]
        return rcopy(src, lead.at[b], sem, l_recv.at[b], up if is_up else down)

    def l_side(b):
        return rcopy(lead.at[b], lead.at[b], lp_send.at[b], lp_recv.at[b], partner)

    def l_start(b):
        for own, cond in ((2, has_prev), (1, jnp.logical_not(has_prev))):
            @pl.when((z == origin[b]) & (core == carrier[b]) & cond)
            def _():
                if origin[b] > 0:
                    l_copy(b, own, False).start()

                @pl.when(has_up)
                def _():
                    l_copy(b, own, True).start()

    def l_relay(b):
        @pl.when((z != origin[b]) & (core == carrier[b]))
        def _():
            l_copy(b, 0, True).wait_recv()

            @pl.when((z > origin[b]) & has_up)
            def _():
                l_copy(b, 0, True).start()
            l_side(b).start()

        @pl.when((z != origin[b]) & (core != carrier[b]))
        def _():
            l_side(b).wait_recv()

    n_x = blocks * PIECES
    for t in range(PIECES):
        x_piece(t)
    for b in range(3):
        l_start(b)
    for u in range(n_r):
        r_start(u)
    for t in range(PIECES, 2 * PIECES):
        x_piece(t)
    for b in range(3):
        l_relay(b)
    plan = [functools.partial(r_relay, k, u) for u in range(n_r) for k in range(2)]
    for t in range(2 * PIECES, n_x):
        x_piece(t)
        if plan:
            plan.pop(0)()
        if plan:
            plan.pop(0)()
    for job in plan:
        job()

    for t in range(n_x):
        a, d = part(t)
        other = cols.at[1 - core, a, d]
        rcopy(other, other, p_send.at[t], p_recv.at[t], partner).wait_recv()
    for t in range(n_x):
        chain, side = x_copies(t, False)
        side.wait_send()

        @pl.when(has_next)
        def _():
            chain.wait_send()
    for u in range(n_r):
        @pl.when(has_up)
        def _():
            r_copy(0, u, False, True).wait_send()

        @pl.when(has_up & (z > 0))
        def _():
            r_copy(1, u, False, True).wait_send()

        @pl.when(z == 1)
        def _():
            r_copy(1, u, False, False).wait_send()
    for b in range(3):
        @pl.when((core == carrier[b]) & (z >= origin[b]) & has_up)
        def _():
            l_copy(b, 0, True).wait_send()

        @pl.when((core == carrier[b]) & (z != origin[b]))
        def _():
            l_side(b).wait_send()
        if origin[b] > 0:
            @pl.when((core == carrier[b]) & (z == origin[b]))
            def _():
                l_copy(b, 0, False).wait_send()

    @pl.when(jnp.logical_not(has_prev))
    def _():
        for a in range(blocks):
            cols[core, a] = m_ref[a, 0]

    for k in range(2):
        @pl.when(z == k)
        def _():
            rows[k] = m_ref[0]
    for b in range(3):
        @pl.when(z == origin[b])
        def _():
            lead[b] = cols[carrier[b], 0]


def factor_small(s_ref):
    n = s_ref.shape[0]
    lane = lax.broadcasted_iota(jnp.int32, (GROUP, n), 1)

    def step(i, carry):
        base = pl.multiple_of(i * GROUP, GROUP)
        g = s_ref[pl.ds(base, GROUP), :]
        diag = pltpu.roll(g[:, :n], lax.rem(n - base, n), 1)
        t = {}
        for a in range(GROUP):
            for b in range(a + 1):
                t[a, b] = jnp.broadcast_to(diag[b:b + 1, a:a + 1], (1, n))
        left = [g[a:a + 1, :n] for a in range(GROUP)]
        right = [g[a:a + 1, n:] for a in range(GROUP)]
        for k in range(GROUP):
            r = lax.rsqrt(t[k, k])
            left[k] = left[k] * r
            right[k] = right[k] * r
            col = {a: t[a, k] * r for a in range(k + 1, GROUP)}
            for a in range(k + 1, GROUP):
                for b in range(k + 1, a + 1):
                    t[a, b] = t[a, b] - col[a] * col[b]
            for a in range(k + 1, GROUP):
                left[a] = left[a] - col[a] * left[k]
                right[a] = right[a] - col[a] * right[k]
        u = jnp.concatenate(left, axis=0)
        v = jnp.concatenate(right, axis=0)
        done = jnp.concatenate([u, v], axis=1)
        s_ref[pl.ds(base, GROUP), :] = done

        def split(w):
            h = w.astype(jnp.bfloat16).astype(jnp.float32)
            rest = w - h
            m = rest.astype(jnp.bfloat16).astype(jnp.float32)
            return h, m, rest - m

        h, m, l = split(done)
        keep = lane >= base + GROUP
        hm, mm_, lm = (jnp.where(keep, w[:, :n], 0.0) for w in (h, m, l))
        lhs = jnp.concatenate([hm, hm, mm_, hm, lm, mm_], axis=0).astype(jnp.bfloat16)
        rhs = jnp.concatenate([h, m, h, l, h, m], axis=0).astype(jnp.bfloat16)
        s_ref[...] -= lax.dot_general(
            lhs, rhs, (((0,), (0,)), ((), ())), preferred_element_type=jnp.float32
        )
        return carry

    lax.fori_loop(0, n // GROUP, step, 0)


def factor(src, low, inv, s_ref):
    size = src.shape[0]
    n = s_ref.shape[0]
    row = lax.broadcasted_iota(jnp.int32, (n, n), 0)
    lane = lax.broadcasted_iota(jnp.int32, (n, n), 1)
    eye = jnp.where(row == lane, 1.0, 0.0)
    low[...] = jnp.zeros_like(low)
    inv[...] = jnp.zeros_like(inv)
    for b in range(size // n):
        at = slice(b * n, (b + 1) * n)
        s_ref[:, :n] = src[at, at]
        s_ref[:, n:] = eye
        factor_small(s_ref)
        v = jnp.where(row >= lane, s_ref[:, n:], 0.0)
        low[at, at] = jnp.where(row <= lane, s_ref[:, :n], 0.0).T
        inv[at, at] = v
        if b > 0:
            inv[at, :b * n] = -mm(v, mm(low[at, :b * n], inv[:b * n, :b * n]))
        if (b + 1) * n < size:
            below = mm_nt(src[(b + 1) * n:, at], v)
            low[(b + 1) * n:, at] = below
            src[(b + 1) * n:, (b + 1) * n:] -= mm_nt(below, below)


def compute(shape, m_ref, cols, rows, lead, out, work, low, inv, l10, q, s_ref):
    n_row, n_col = shape
    z = lax.axis_index("row")
    col = lax.axis_index("col")
    blocks, per = m_ref.shape[0], m_ref.shape[1]
    work[...] = lead[0]
    factor(work, low.at[0], inv.at[0], s_ref)
    l10[...] = mm_nt(lead[1], inv[0])
    work[...] = lead[2] - mm_nt(l10[...], l10[...])
    factor(work, low.at[1], inv.at[1], s_ref)
    for c in range(per):
        q[0, c] = mm(inv[0], rows[0, c])
        q[1, c] = mm(inv[1], rows[1, c] - mm(l10[...], q[0, c]))

    def block_row(a, carry):
        p0 = mm_nt(cols[0, a], inv[0])
        p1 = mm_nt(cols[1, a] - mm_nt(p0, l10[...]), inv[1])
        for c in range(per):
            out[a, c] = m_ref[a, c] - mm(p0, q[0, c]) - mm(p1, q[1, c])

        @pl.when(col == 0)
        def _():
            out[a, 0] = p0

        @pl.when(col == 1)
        def _():
            out[a, 0] = p1
        return carry

    lax.fori_loop(0, blocks, block_row, 0)

    @pl.when(z < PANELS)
    def _():
        out[0] = jnp.zeros_like(out[0])

        @pl.when((z == 0) & (col == 0))
        def _():
            out[0, 0] = low[0]

        @pl.when((z == 1) & (col == 0))
        def _():
            out[0, 0] = l10[...]

        @pl.when((z == 1) & (col == 1))
        def _():
            out[0, 0] = low[1]


def shards(shape, matrix):
    m = matrix.transpose(0, 2, 1, 3)
    blocks, per, size, _ = m.shape
    f32 = jnp.float32
    dma = pltpu.SemaphoreType.DMA
    n_x, n_r = blocks * PIECES, per * PIECES
    vmem = pl.BlockSpec(memory_space=pltpu.VMEM)
    cols, rows, lead = pl.pallas_call(
        functools.partial(exchange, shape),
        out_shape=(jax.ShapeDtypeStruct((2, blocks, size, size), f32),
                   jax.ShapeDtypeStruct((2, per, size, size), f32),
                   jax.ShapeDtypeStruct((3, size, size), f32)),
        in_specs=[vmem],
        out_specs=(vmem, vmem, vmem),
        scratch_shapes=[dma((n_x,))] * 4 + [dma((3,))] * 5 + [dma((2, n_r)), dma((n_r,)), dma((2, n_r))],
        compiler_params=pltpu.CompilerParams(collective_id=0, has_side_effects=True),
        name="exchange",
    )(m)
    tile = 128
    out = pl.pallas_call(
        functools.partial(compute, shape),
        out_shape=jax.ShapeDtypeStruct(m.shape, f32),
        in_specs=[vmem] * 4,
        out_specs=vmem,
        scratch_shapes=[
            pltpu.VMEM((size, size), f32),
            pltpu.VMEM((2, size, size), f32),
            pltpu.VMEM((2, size, size), f32),
            pltpu.VMEM((size, size), f32),
            pltpu.VMEM((2, per, size, size), f32),
            pltpu.VMEM((tile, 2 * tile), f32),
        ],
        name="compute",
    )(m, cols, rows, lead)
    return out.transpose(0, 2, 1, 3)


def solution(mesh):
    spec = P(None, "row", None, "col")
    shape = (mesh.shape["row"], mesh.shape["col"])
    return jax.shard_map(
        functools.partial(shards, shape), mesh=mesh, in_specs=(spec,), out_specs=spec, check_vma=False
    )
```

time: 442 us -> 125 us (0.28)
  the two profiles are of different devices: /device:TPU:0 before, /device:TPU:28 now
where the time goes in v1:
time: 125 us; the launch traced here: 124 us
  Pallas kernels  117 us (94%)
  local copies, waits for them, and re-layouts  7.64 us (6%)
    pallas_call x1, Pallas kernels, shards(): pl.pallas_call(functools.partial(exchange, shape), out_shape=(jax.ShapeDt...  71.5 us
    pallas_call x1, Pallas kernels, shards(): pl.pallas_call(functools.partial(compute, shape), out_shape=jax.ShapeDtyp...  45.2 us
    transpose x1, local copies, waits for them, and re-layouts, shards(): return out.transpose(0, 2, 1, 3)  4.53 us
    unnamed x1, local copies, waits for them, and re-layouts  3.11 us

profile of v1, /device:TPU:28, one launch (start us, length us, event | category | flops | bytes accessed | tf_op | source)
XLA Modules:
  0.0 124.4 jit_solution(16951870703357838617)
XLA Ops:
  0.0 3.1 %copy.5 = f32[4,256,2,256]{3,1,2,0:T(8,128)} copy(f32[4,256,2,256]{3,2,1,0:T(2,128)} %param.1) | data formatting | bytes 4194304 | tf_op args[0]
  3.1 71.5 %exchange.1 = (f32[2,4,256,256]{3,2,1,0:T(8,128)}, f32[2,2,256,256]{3,2,1,0:T(8,128)}, f32[3,256,256]{2,1,0:T(8,128)}) custom-call(f32[4,2,256,256]{3,2,1,0:T(8,128)} %bitcast.4), custom_call_target="tpu_custom_call" | custom-call | tf_op jit(solution)/shard_map/exchange/pallas_call | solution.py:384
  74.6 45.2 %compute.1 = f32[4,2,256,256]{3,2,1,0:T(8,128)} custom-call(f32[4,2,256,256]{3,2,1,0:T(8,128)} %bitcast.5, f32[2,4,256,256]{3,2,1,0:T(8,128)} %get-tuple-element.8.cols, f32[2,2,256,256]{3,2,1,0:T(8,128)} %get-tuple-element.9.rows, f32[3,256,256]{2,1,0:T(8,128)} %get-tuple-element.10.lead), custom_call_target="tpu_custom_call" | custom-call | tf_op jit(solution)/shard_map/compute/pallas_call | solution.py:396
  119.8 4.5 %copy.3 = f32[4,256,2,256]{3,2,1,0:T(2,128)} copy(f32[4,256,2,256]{3,1,2,0:T(8,128)} %bitcast.6) | data formatting | bytes 4194304 | tf_op jit(solution)/shard_map/transpose | solution.py:411

commit v2 on v1

v2 whole, which is shorter than its diff:
```python
import functools
import math

import jax
import jax.numpy as jnp
from jax import lax
from jax.experimental import pallas as pl
from jax.experimental.pallas import tpu as pltpu
from jax.sharding import PartitionSpec as P

MESH = pl.DeviceIdType.MESH
PANELS = 2
PIECES = 4
R_PIECES = 2
STEPS = 4
GROUP = 8
HIGHEST = lax.Precision.HIGHEST


def mm(a, b):
    return jnp.dot(a, b, precision=HIGHEST, preferred_element_type=jnp.float32)


def mm_nt(a, b):
    return lax.dot_general(
        a, b, (((1,), (1,)), ((), ())), precision=HIGHEST, preferred_element_type=jnp.float32
    )


def mm_tn(a, b):
    return lax.dot_general(
        a, b, (((0,), (0,)), ((), ())), precision=HIGHEST, preferred_element_type=jnp.float32
    )


def snake(pos, width):
    major, minor = pos // width, pos % width
    return major, jnp.where(major % 2 == 0, minor, width - 1 - minor)


class Exchange:
    def __init__(self, shape, m_ref, cols, rows, lead, sems):
        (self.x_send, self.x_recv, self.p_send, self.p_recv, self.l_up, self.l_down, self.l_side,
         self.l_recv, self.lp_send, self.lp_recv, self.r_up, self.r_down, self.r_recv) = sems
        self.m, self.cols, self.rows, self.lead = m_ref, cols, rows, lead
        n_row, n_col = shape
        self.n_row, self.n_col = shape
        chips = n_col // 2
        width = math.isqrt(chips)
        if width * width != chips:
            width = chips
        height = chips // width
        z = lax.axis_index("row")
        col = lax.axis_index("col")
        chip, core = col // 2, col % 2
        y, x = chip // width, chip % width
        pos_a = y * width + jnp.where(y % 2 == 0, x, width - 1 - x)
        pos_b = x * height + jnp.where(x % 2 == 0, y, height - 1 - y)
        pos = jnp.where(core == 0, pos_a, pos_b)

        def chip_at(p):
            ya, xa = snake(p, width)
            xb, yb = snake(p, height)
            return jnp.where(core == 0, ya * width + xa, yb * width + xb)

        last = chips - 1
        self.z, self.col, self.core = z, col, core
        self.odd = chip % 2 == 1
        self.partner = (z, chip * 2 + 1 - core)
        self.beside = (z, (chip + 1 - 2 * (chip % 2)) * 2 + core)
        self.has_next, self.has_prev = pos < last, pos > 0
        self.nxt = (z, chip_at(jnp.minimum(pos + 1, last)) * 2 + core)
        prv = (z, chip_at(jnp.maximum(pos - 1, 0)) * 2 + core)
        self.up, self.down = (z + 1, col), (z - 1, col)
        self.has_up, has_down = z < n_row - 1, z > 0
        self.blocks, self.per, self.size = m_ref.shape[0], m_ref.shape[1], m_ref.shape[2]
        self.n_x = self.blocks * PIECES
        self.n_r = self.per * R_PIECES
        self.home = col % n_row
        self.late = self.home >= PANELS

        barrier = pltpu.get_barrier_semaphore()

        def greet(cond, dev):
            @pl.when(cond)
            def _():
                pl.semaphore_signal(barrier, inc=1, device_id=dev, device_id_type=MESH)

        for dev in (self.partner, self.beside):
            pl.semaphore_signal(barrier, inc=1, device_id=dev, device_id_type=MESH)
        near = ((self.has_next, self.nxt), (self.has_prev, prv), (self.has_up, self.up),
                (has_down, self.down))
        count = 2
        for cond, dev in near:
            greet(cond, dev)
            count = count + jnp.where(cond, 1, 0)
        pl.semaphore_wait(barrier, count)

    def copy(self, src, dst, s, r, dev):
        return pltpu.make_async_remote_copy(
            src_ref=src, dst_ref=dst, send_sem=s, recv_sem=r, device_id=dev, device_id_type=MESH
        )

    def part(self, t, pieces):
        step = self.size // pieces
        return t // pieces, pl.ds((t % pieces) * step, step)

    def x_copies(self, t, own):
        a, d = self.part(t, PIECES)
        dst = self.cols.at[self.core, a, d]
        src = self.m.at[a, 0, d] if own else dst
        return (self.copy(src, dst, self.x_send.at[t], self.x_recv.at[t], self.nxt),
                self.copy(src, dst, self.p_send.at[t], self.p_recv.at[t], self.partner))

    def x_piece(self, t):
        @pl.when(jnp.logical_not(self.has_prev))
        def _():
            chain, side = self.x_copies(t, True)
            chain.start()
            side.start()

        @pl.when(self.has_prev)
        def _():
            chain, side = self.x_copies(t, False)
            chain.wait_recv()

            @pl.when(self.has_next)
            def _():
                chain.start()
            side.start()

    def x_other(self, t):
        a, d = self.part(t, PIECES)
        ref = self.cols.at[1 - self.core, a, d]
        self.copy(ref, ref, self.p_send.at[t], self.p_recv.at[t], self.partner).wait_recv()

    def r_copy(self, k, u, src, is_up):
        c, d = self.part(u, R_PIECES)
        dst = self.rows.at[k, c, d]
        ref = {"own": lambda: self.m.at[0, c, d],
               "column": lambda: self.cols.at[k, (c * self.n_col + self.col) // self.n_row, d],
               "relay": lambda: dst}[src]()
        sem = (self.r_up if is_up else self.r_down).at[k, u]
        return self.copy(ref, dst, sem, self.r_recv.at[k, u], self.up if is_up else self.down)

    def r_roles(self, k):
        z, late, home = self.z, self.late, self.home
        early = jnp.logical_not(late)
        top = self.n_row - 1
        own_up = (z == k) & jnp.where(late, z + 1 < PANELS, z < top)
        own_down = (z == k) & (z > 0)
        column = late & (z == home)
        column_up = column & (z < top)
        column_down = column & (z > PANELS)
        relay_up = (early & (z > k) & (z < top)) | (late & (z > home) & (z < top))
        relay_down = late & (z > PANELS) & (z < home)
        arrives = jnp.where(late & (z >= PANELS), z != home, z != k)
        return own_up, own_down, column_up, column_down, relay_up, relay_down, arrives

    def r_begin(self):
        for k in range(PANELS):
            own_up, own_down, *_ = self.r_roles(k)
            for u in range(self.n_r):
                if k == 0 or u < self.n_r // 2:
                    @pl.when(own_up)
                    def _():
                        self.r_copy(k, u, "own", True).start()

                @pl.when(own_down)
                def _():
                    self.r_copy(k, u, "own", False).start()

    def r_piece(self, k, u):
        own_up, _, column_up, column_down, relay_up, relay_down, arrives = self.r_roles(k)
        if not (k == 0 or u < self.n_r // 2):
            @pl.when(own_up)
            def _():
                self.r_copy(k, u, "own", True).start()

        @pl.when(arrives)
        def _():
            self.r_copy(k, u, "relay", True).wait_recv()
        for cond, src, is_up in ((column_up, "column", True), (column_down, "column", False),
                                 (relay_up, "relay", True), (relay_down, "relay", False)):
            @pl.when(cond)
            def _():
                self.r_copy(k, u, src, is_up).start()

    ORIGIN = (0, 1, 1)
    CARRIER = (0, 0, 1)

    def l_copy(self, b, q, own, way):
        _, d = self.part(q, PIECES)
        dst = self.lead.at[b, d]
        src = self.cols.at[self.CARRIER[b], 0, d] if own else dst
        sem, dev = {"up": (self.l_up, self.up), "down": (self.l_down, self.down),
                    "beside": (self.l_side, self.beside)}[way]
        return self.copy(src, dst, sem.at[b, q], self.l_recv.at[b, q], dev)

    def l_partner(self, b, q):
        _, d = self.part(q, PIECES)
        ref = self.lead.at[b, d]
        return self.copy(ref, ref, self.lp_send.at[b, q], self.lp_recv.at[b, q], self.partner)

    def l_start(self, b, q):
        @pl.when((self.z == self.ORIGIN[b]) & (self.core == self.CARRIER[b]) & self.odd)
        def _():
            if self.ORIGIN[b] > 0:
                self.l_copy(b, q, True, "down").start()

            @pl.when(self.has_up)
            def _():
                self.l_copy(b, q, True, "up").start()

    def l_relay(self, b, q):
        away = self.z != self.ORIGIN[b]
        mine = self.core == self.CARRIER[b]

        @pl.when(away & mine)
        def _():
            self.l_copy(b, q, False, "up").wait_recv()

            @pl.when(self.odd)
            def _():
                @pl.when((self.z > self.ORIGIN[b]) & self.has_up)
                def _():
                    self.l_copy(b, q, False, "up").start()
                self.l_copy(b, q, False, "beside").start()
            self.l_partner(b, q).start()

        @pl.when(away & jnp.logical_not(mine))
        def _():
            self.l_partner(b, q).wait_recv()

    def drain(self):
        for t in range(self.n_x):
            chain, side = self.x_copies(t, False)
            side.wait_send()

            @pl.when(self.has_next)
            def _():
                chain.wait_send()
        for k in range(PANELS):
            own_up, own_down, column_up, column_down, relay_up, relay_down, _ = self.r_roles(k)
            for u in range(self.n_r):
                @pl.when(own_up | column_up | relay_up)
                def _():
                    self.r_copy(k, u, "relay", True).wait_send()

                @pl.when(own_down | column_down | relay_down)
                def _():
                    self.r_copy(k, u, "relay", False).wait_send()
        for b in range(3):
            mine = self.core == self.CARRIER[b]
            away = self.z != self.ORIGIN[b]
            for q in range(PIECES):
                @pl.when(mine & self.odd & (self.z >= self.ORIGIN[b]) & self.has_up)
                def _():
                    self.l_copy(b, q, False, "up").wait_send()
                if self.ORIGIN[b] > 0:
                    @pl.when(mine & self.odd & (self.z == self.ORIGIN[b]))
                    def _():
                        self.l_copy(b, q, False, "down").wait_send()

                @pl.when(mine & self.odd & away)
                def _():
                    self.l_copy(b, q, False, "beside").wait_send()

                @pl.when(mine & away)
                def _():
                    self.l_partner(b, q).wait_send()


def factor_small(s_ref, hook):
    n = s_ref.shape[0]
    lane = lax.broadcasted_iota(jnp.int32, (GROUP, n), 1)

    def step(i, carry):
        base = pl.multiple_of(i * GROUP, GROUP)
        g = s_ref[pl.ds(base, GROUP), :]
        diag = pltpu.roll(g[:, :n], lax.rem(n - base, n), 1)
        t = {}
        for a in range(GROUP):
            for b in range(a + 1):
                t[a, b] = jnp.broadcast_to(diag[b:b + 1, a:a + 1], (1, n))
        left = [g[a:a + 1, :n] for a in range(GROUP)]
        right = [g[a:a + 1, n:] for a in range(GROUP)]
        for k in range(GROUP):
            r = lax.rsqrt(t[k, k])
            left[k] = left[k] * r
            right[k] = right[k] * r
            col = {a: t[a, k] * r for a in range(k + 1, GROUP)}
            for a in range(k + 1, GROUP):
                for b in range(k + 1, a + 1):
                    t[a, b] = t[a, b] - col[a] * col[b]
            for a in range(k + 1, GROUP):
                left[a] = left[a] - col[a] * left[k]
                right[a] = right[a] - col[a] * right[k]
        u = jnp.concatenate(left, axis=0)
        v = jnp.concatenate(right, axis=0)
        done = jnp.concatenate([u, v], axis=1)
        s_ref[pl.ds(base, GROUP), :] = done

        def split(w):
            h = w.astype(jnp.bfloat16).astype(jnp.float32)
            rest = w - h
            m = rest.astype(jnp.bfloat16).astype(jnp.float32)
            return h, m, rest - m

        h, m, l = split(done)
        keep = lane >= base + GROUP
        hm, mm_, lm = (jnp.where(keep, w[:, :n], 0.0) for w in (h, m, l))
        lhs = jnp.concatenate([hm, hm, mm_, hm, lm, mm_], axis=0).astype(jnp.bfloat16)
        rhs = jnp.concatenate([h, m, h, l, h, m], axis=0).astype(jnp.bfloat16)
        s_ref[...] -= lax.dot_general(
            lhs, rhs, (((0,), (0,)), ((), ())), preferred_element_type=jnp.float32
        )
        return carry

    for start in range(0, n // GROUP, STEPS):
        hook()
        lax.fori_loop(start, min(start + STEPS, n // GROUP), step, 0)


def factor(src, low, inv, s_ref, hook):
    size = src.shape[0]
    n = s_ref.shape[0]
    row = lax.broadcasted_iota(jnp.int32, (n, n), 0)
    lane = lax.broadcasted_iota(jnp.int32, (n, n), 1)
    eye = jnp.where(row == lane, 1.0, 0.0)
    low[...] = jnp.zeros_like(low)
    inv[...] = jnp.zeros_like(inv)
    for b in range(size // n):
        at = slice(b * n, (b + 1) * n)
        s_ref[:, :n] = src[at, at]
        s_ref[:, n:] = eye
        factor_small(s_ref, hook)
        v = jnp.where(row >= lane, s_ref[:, n:], 0.0)
        low[at, at] = jnp.where(row <= lane, s_ref[:, :n], 0.0).T
        inv[at, at] = v
        if b > 0:
            inv[at, :b * n] = -mm(v, mm(low[at, :b * n], inv[:b * n, :b * n]))
        if (b + 1) * n < size:
            below = mm_nt(src[(b + 1) * n:, at], v)
            low[(b + 1) * n:, at] = below
            src[(b + 1) * n:, (b + 1) * n:] -= mm_nt(below, below)


def hooks(ex):
    every = [[] for _ in range(16)]
    for q in range(PIECES):
        every[q] += [functools.partial(ex.l_relay, 1, q), functools.partial(ex.l_relay, 2, q)]
    for i, t in enumerate(range(2 * PIECES, ex.n_x)):
        every[min(i * 3 // 4, 7)].append(functools.partial(ex.x_piece, t))
    for i, t in enumerate(range(PIECES, ex.n_x)):
        every[min(i * 3 // 4, 8)].append(functools.partial(ex.x_other, t))
    half = ex.n_r // 2
    order = [(k, h * half + u) for h in range(2) for k in (1, 0) for u in range(half)]
    when = [0, 2, 4, 6, 9, 11, 13, 15]
    for i, (k, u) in enumerate(order):
        every[when[min(i, 7)]].append(functools.partial(ex.r_piece, k, u))
    return every


def compute(shape, m_ref, out, cols, rows, lead, work, low, inv, l10, q, s_ref, *sems):
    n_row, n_col = shape
    z = lax.axis_index("row")
    col = lax.axis_index("col")
    blocks, per = m_ref.shape[0], m_ref.shape[1]
    ex = Exchange(shape, m_ref, cols, rows, lead, sems)
    for t in range(PIECES):
        ex.x_piece(t)
        for b in range(3):
            ex.l_start(b, t)
    ex.r_begin()

    @pl.when(jnp.logical_not(ex.has_prev))
    def _():
        for a in range(blocks):
            cols[ex.core, a] = m_ref[a, 0]

    for t in range(PIECES):
        ex.x_other(t)
    for t in range(PIECES):
        ex.l_relay(0, t)
        ex.x_piece(PIECES + t)
    todo = hooks(ex)

    def hook():
        if todo:
            for job in todo.pop(0):
                job()

    def leading(b):
        @pl.when(z == ex.ORIGIN[b])
        def _():
            lead[b] = cols[ex.CARRIER[b], 0]
        return lead[b]

    work[...] = leading(0)
    factor(work, low.at[0], inv.at[0], s_ref, hook)
    l10[...] = mm_nt(leading(1), inv[0])
    work[...] = leading(2) - mm_nt(l10[...], l10[...])
    factor(work, low.at[1], inv.at[1], s_ref, hook)
    while todo:
        hook()

    for k in range(PANELS):
        turned = ex.late & (z >= PANELS)

        @pl.when(z == k)
        def _():
            q[k] = m_ref[0]

        @pl.when((z != k) & jnp.logical_not(turned))
        def _():
            q[k] = rows[k]
        for c in range(per):
            @pl.when(turned & (z == ex.home))
            def _():
                q[k, c] = cols[k, (c * n_col + col) // n_row].T

            @pl.when(turned & (z != ex.home))
            def _():
                q[k, c] = rows[k, c].T

    for c in range(per):
        q[0, c] = mm(inv[0], q[0, c])
        q[1, c] = mm(inv[1], q[1, c] - mm(l10[...], q[0, c]))

    def block_row(a, carry):
        p0 = mm_nt(cols[0, a], inv[0])
        p1 = mm_nt(cols[1, a] - mm_nt(p0, l10[...]), inv[1])
        for c in range(per):
            out[a, c] = m_ref[a, c] - mm(p0, q[0, c]) - mm(p1, q[1, c])

        @pl.when(col == 0)
        def _():
            out[a, 0] = p0

        @pl.when(col == 1)
        def _():
            out[a, 0] = p1
        return carry

    lax.fori_loop(0, blocks, block_row, 0)

    @pl.when(z < PANELS)
    def _():
        out[0] = jnp.zeros_like(out[0])

        @pl.when((z == 0) & (col == 0))
        def _():
            out[0, 0] = low[0]

        @pl.when((z == 1) & (col == 0))
        def _():
            out[0, 0] = l10[...]

        @pl.when((z == 1) & (col == 1))
        def _():
            out[0, 0] = low[1]
    ex.drain()


def shards(shape, matrix):
    m = matrix.transpose(0, 2, 1, 3)
    blocks, per, size, _ = m.shape
    f32 = jnp.float32
    dma = pltpu.SemaphoreType.DMA
    n_x, n_r = blocks * PIECES, per * R_PIECES
    tile = 128
    vmem = pl.BlockSpec(memory_space=pltpu.VMEM)
    out = pl.pallas_call(
        functools.partial(compute, shape),
        out_shape=jax.ShapeDtypeStruct(m.shape, f32),
        in_specs=[vmem],
        out_specs=vmem,
        scratch_shapes=[
            pltpu.VMEM((PANELS, blocks, size, size), f32),
            pltpu.VMEM((PANELS, per, size, size), f32),
            pltpu.VMEM((3, size, size), f32),
            pltpu.VMEM((size, size), f32),
            pltpu.VMEM((PANELS, size, size), f32),
            pltpu.VMEM((PANELS, size, size), f32),
            pltpu.VMEM((size, size), f32),
            pltpu.VMEM((PANELS, per, size, size), f32),
            pltpu.VMEM((tile, 2 * tile), f32),
        ] + [dma((n_x,))] * 4 + [dma((3, PIECES))] * 6 + [dma((PANELS, n_r))] * 3,
        compiler_params=pltpu.CompilerParams(collective_id=0, has_side_effects=True),
        name="factor",
    )(m)
    return out.transpose(0, 2, 1, 3)


def solution(mesh):
    spec = P(None, "row", None, "col")
    shape = (mesh.shape["row"], mesh.shape["col"])
    return jax.shard_map(
        functools.partial(shards, shape), mesh=mesh, in_specs=(spec,), out_specs=spec, check_vma=False
    )
```

time: 125 us -> 161 us (1.29)
  Pallas kernels: 117 us -> 153 us
    pallas_call x1, Pallas kernels: 45.2 us -> 153 us  [shards(): pl.pallas_call(functools.partial(compute, shape), out_shape=jax.ShapeDtyp...]
    pallas_call x1 -> x0, Pallas kernels: 71.5 us -> none  [shards(): pl.pallas_call(functools.partial(exchange, shape), out_shape=(jax.ShapeDt...]
where the time goes in v2:
time: 161 us
  Pallas kernels  153 us (95%)
  local copies, waits for them, and re-layouts  7.64 us (5%)
    pallas_call x1, Pallas kernels, shards(): pl.pallas_call(functools.partial(compute, shape), out_shape=jax.ShapeDtyp...  153 us
    transpose x1, local copies, waits for them, and re-layouts, shards(): return out.transpose(0, 2, 1, 3)  4.53 us

profile of v2, /device:TPU:28, one launch (start us, length us, event | category | flops | bytes accessed | tf_op | source)
XLA Modules:
  0.0 160.7 jit_solution(13965705126328707228)
XLA Ops:
  0.0 3.1 %copy.5 = f32[4,256,2,256]{3,1,2,0:T(8,128)} copy(f32[4,256,2,256]{3,2,1,0:T(2,128)} %param.1) | data formatting | bytes 4194304 | tf_op args[0]
  3.1 153.0 %factor.1 = f32[4,2,256,256]{3,2,1,0:T(8,128)} custom-call(f32[4,2,256,256]{3,2,1,0:T(8,128)} %bitcast.5), custom_call_target="tpu_custom_call" | custom-call | tf_op jit(solution)/shard_map/factor/pallas_call | solution.py:474
  156.1 4.5 %copy.3 = f32[4,256,2,256]{3,2,1,0:T(2,128)} copy(f32[4,256,2,256]{3,1,2,0:T(8,128)} %bitcast.4) | data formatting | bytes 4194304 | tf_op jit(solution)/shard_map/transpose | solution.py:493

commit v3 on v2

--- a/solution.py
+++ b/solution.py
@@ -112,13 +112,14 @@
         return (self.copy(src, dst, self.x_send.at[t], self.x_recv.at[t], self.nxt),
                 self.copy(src, dst, self.p_send.at[t], self.p_recv.at[t], self.partner))
 
-    def x_piece(self, t):
+    def x_begin(self, t):
         @pl.when(jnp.logical_not(self.has_prev))
         def _():
             chain, side = self.x_copies(t, True)
             chain.start()
             side.start()
 
+    def x_piece(self, t):
         @pl.when(self.has_prev)
         def _():
             chain, side = self.x_copies(t, False)
@@ -157,25 +158,22 @@
         arrives = jnp.where(late & (z >= PANELS), z != home, z != k)
         return own_up, own_down, column_up, column_down, relay_up, relay_down, arrives
 
-    def r_begin(self):
+    def r_begin(self, cond):
         for k in range(PANELS):
             own_up, own_down, *_ = self.r_roles(k)
             for u in range(self.n_r):
-                if k == 0 or u < self.n_r // 2:
-                    @pl.when(own_up)
-                    def _():
-                        self.r_copy(k, u, "own", True).start()
-
-                @pl.when(own_down)
+                @pl.when(own_up & cond)
+                def _():
+                    self.r_copy(k, u, "own", True).start()
+
+                @pl.when(own_down & cond)
                 def _():
                     self.r_copy(k, u, "own", False).start()
 
-    def r_piece(self, k, u):
-        own_up, _, column_up, column_down, relay_up, relay_down, arrives = self.r_roles(k)
-        if not (k == 0 or u < self.n_r // 2):
-            @pl.when(own_up)
-            def _():
-                self.r_copy(k, u, "own", True).start()
+    def r_piece(self, k, u, cond):
+        _, _, column_up, column_down, relay_up, relay_down, arrives = (
+            role & cond for role in self.r_roles(k)
+        )
 
         @pl.when(arrives)
         def _():
@@ -348,17 +346,21 @@
 
 def hooks(ex):
     every = [[] for _ in range(16)]
-    for q in range(PIECES):
-        every[q] += [functools.partial(ex.l_relay, 1, q), functools.partial(ex.l_relay, 2, q)]
-    for i, t in enumerate(range(2 * PIECES, ex.n_x)):
-        every[min(i * 3 // 4, 7)].append(functools.partial(ex.x_piece, t))
     for i, t in enumerate(range(PIECES, ex.n_x)):
-        every[min(i * 3 // 4, 8)].append(functools.partial(ex.x_other, t))
+        every[min(i // 2, 7)].append(functools.partial(ex.x_piece, t))
+        every[min(i // 2 + 1, 8)].append(functools.partial(ex.x_other, t))
     half = ex.n_r // 2
     order = [(k, h * half + u) for h in range(2) for k in (1, 0) for u in range(half)]
-    when = [0, 2, 4, 6, 9, 11, 13, 15]
-    for i, (k, u) in enumerate(order):
-        every[when[min(i, 7)]].append(functools.partial(ex.r_piece, k, u))
+    first = ex.z < PANELS
+    classes = (
+        (jnp.logical_not(ex.late) & first, (0,) * 8),
+        (jnp.logical_not(ex.late) & jnp.logical_not(first), (1, 2, 6, 7, 2, 3, 9, 12)),
+        (ex.late & first, (6,) * 8),
+        (ex.late & jnp.logical_not(first), (3, 3, 4, 4, 8, 8, 9, 9)),
+    )
+    for cond, when in classes:
+        for i, (k, u) in enumerate(order):
+            every[when[min(i, 7)]].append(functools.partial(ex.r_piece, k, u, cond))
     return every
 
 
@@ -368,22 +370,25 @@
     col = lax.axis_index("col")
     blocks, per = m_ref.shape[0], m_ref.shape[1]
     ex = Exchange(shape, m_ref, cols, rows, lead, sems)
+    for t in range(ex.n_x):
+        ex.x_begin(t)
+    ex.r_begin(jnp.logical_not(ex.late))
     for t in range(PIECES):
         ex.x_piece(t)
         for b in range(3):
             ex.l_start(b, t)
-    ex.r_begin()
 
     @pl.when(jnp.logical_not(ex.has_prev))
     def _():
         for a in range(blocks):
             cols[ex.core, a] = m_ref[a, 0]
 
+    for b in range(3):
+        for t in range(PIECES):
+            ex.l_relay(b, t)
+    ex.r_begin(ex.late)
     for t in range(PIECES):
         ex.x_other(t)
-    for t in range(PIECES):
-        ex.l_relay(0, t)
-        ex.x_piece(PIECES + t)
     todo = hooks(ex)
 
     def hook():

time: 161 us -> 123 us (0.76)
  the two profiles are of different devices: /device:TPU:28 before, /device:TPU:26 now
where the time goes in v3:
time: 123 us
  Pallas kernels  115 us (93%)
  local copies, waits for them, and re-layouts  7.64 us (6%)
    pallas_call x1, Pallas kernels, shards(): pl.pallas_call(functools.partial(compute, shape), out_shape=jax.ShapeDtyp...  115 us
    transpose x1, local copies, waits for them, and re-layouts, shards(): return out.transpose(0, 2, 1, 3)  4.53 us
    unnamed x1, local copies, waits for them, and re-layouts  3.11 us

profile of v3, /device:TPU:26, one launch (start us, length us, event | category | flops | bytes accessed | tf_op | source)
XLA Modules:
  0.0 122.6 jit_solution(4479549839749879803)
XLA Ops:
  0.0 3.1 %copy.5 = f32[4,256,2,256]{3,1,2,0:T(8,128)} copy(f32[4,256,2,256]{3,2,1,0:T(2,128)} %param.1) | data formatting | bytes 4194304 | tf_op args[0]
  3.1 115.0 %factor.1 = f32[4,2,256,256]{3,2,1,0:T(8,128)} custom-call(f32[4,2,256,256]{3,2,1,0:T(8,128)} %bitcast.5), custom_call_target="tpu_custom_call" | custom-call | tf_op jit(solution)/shard_map/factor/pallas_call | solution.py:479
  118.1 4.5 %copy.3 = f32[4,256,2,256]{3,2,1,0:T(2,128)} copy(f32[4,256,2,256]{3,1,2,0:T(8,128)} %bitcast.4) | data formatting | bytes 4194304 | tf_op jit(solution)/shard_map/transpose | solution.py:498

commit v4 on v2

--- a/solution.py
+++ b/solution.py
@@ -348,8 +348,6 @@
 
 def hooks(ex):
     every = [[] for _ in range(16)]
-    for q in range(PIECES):
-        every[q] += [functools.partial(ex.l_relay, 1, q), functools.partial(ex.l_relay, 2, q)]
     for i, t in enumerate(range(2 * PIECES, ex.n_x)):
         every[min(i * 3 // 4, 7)].append(functools.partial(ex.x_piece, t))
     for i, t in enumerate(range(PIECES, ex.n_x)):
@@ -372,8 +370,6 @@
         ex.x_piece(t)
         for b in range(3):
             ex.l_start(b, t)
-    ex.r_begin()
-
     @pl.when(jnp.logical_not(ex.has_prev))
     def _():
         for a in range(blocks):
@@ -383,7 +379,12 @@
         ex.x_other(t)
     for t in range(PIECES):
         ex.l_relay(0, t)
+    for t in range(PIECES):
+        ex.l_relay(1, t)
+        ex.l_relay(2, t)
+    for t in range(PIECES):
         ex.x_piece(PIECES + t)
+    ex.r_begin()
     todo = hooks(ex)
 
     def hook():

time: 161 us -> 107 us (0.66)
  Pallas kernels: 153 us -> 98 us
    pallas_call x1, Pallas kernels: 153 us -> 98 us  [shards(): pl.pallas_call(functools.partial(compute, shape), out_shape=jax.ShapeDtyp...]
where the time goes in v4:
time: 107 us; the launch traced here: 106 us
  Pallas kernels  98 us (92%)
  local copies, waits for them, and re-layouts  7.64 us (7%)
    pallas_call x1, Pallas kernels, shards(): pl.pallas_call(functools.partial(compute, shape), out_shape=jax.ShapeDtyp...  98 us
    transpose x1, local copies, waits for them, and re-layouts, shards(): return out.transpose(0, 2, 1, 3)  4.53 us
    unnamed x1, local copies, waits for them, and re-layouts  3.11 us

profile of v4, /device:TPU:28, one launch (start us, length us, event | category | flops | bytes accessed | tf_op | source)
XLA Modules:
  0.0 105.7 jit_solution(10303889677368769310)
XLA Ops:
  0.0 3.1 %copy.5 = f32[4,256,2,256]{3,1,2,0:T(8,128)} copy(f32[4,256,2,256]{3,2,1,0:T(2,128)} %param.1) | data formatting | bytes 4194304 | tf_op args[0]
  3.1 98.0 %factor.1 = f32[4,2,256,256]{3,2,1,0:T(8,128)} custom-call(f32[4,2,256,256]{3,2,1,0:T(8,128)} %bitcast.5), custom_call_target="tpu_custom_call" | custom-call | tf_op jit(solution)/shard_map/factor/pallas_call | solution.py:475
  101.1 4.5 %copy.3 = f32[4,256,2,256]{3,2,1,0:T(2,128)} copy(f32[4,256,2,256]{3,1,2,0:T(8,128)} %bitcast.4) | data formatting | bytes 4194304 | tf_op jit(solution)/shard_map/transpose | solution.py:494
